TPU v7x, 128 devices: a whole 4x4x4 slice. The times are simulated.
128 devices in a mesh: wide: 8 (over y, core), narrow: 16 (over x, z).
Axes of the slice: x: 4, y: 4, z: 4, core: 2. Of those that a mesh axis runs over, the one named last changes fastest.
Arguments:
- site_basis: bfloat16 [512, 512], P(('wide', 'narrow')), may hold values from -0.25 to 0.25
- left_ops: bfloat16 [384, 512, 512], P(('wide', 'narrow')), may hold values from -0.25 to 0.25
- right_ops: bfloat16 [384, 512, 512], P(('wide', 'narrow')), may hold values from -0.25 to 0.25
- integrals: bfloat16 [384, 384], replicated, may hold values from -0.3125 to 0.3125
- wavefunction: bfloat16 [512, 512], P(('wide', 'narrow')), may hold values from -6 to 6
- pair_order: int32 [384], replicated, may hold values from 0 to 383, each once
- sector_sizes: int32 [8], replicated, may hold values from 1 to 128, 512 in all
Outputs:
- propagated: float32 [512, 512], P(('wide', 'narrow'))
Inputs may be any that keep to these rules, and one draw needn't show every extreme that they name: `pair_order`: each orbital pair stands in exactly one of the 384 slots. `sector_sizes`: the sizes sum to 512.
All inputs are finite; a program needn't handle non-finite values.
Results may differ from a plain program's by a relative error of at most 0.008.
Values may be sent and summed in bfloat16 or wider, within the bound.
A program may use at most 64 MiB of HBM per device.

v0:
```python
import math

import jax
import jax.numpy as jnp
from jax import lax
from jax.sharding import Mesh
from jax.sharding import PartitionSpec as P

ORDER = 3
WIDE_NARROW = ("wide_0", "wide_1", "narrow_0", "narrow_1")


def from_everyone(array, axis):
    length = lax.axis_size(axis)
    return lax.all_to_all(
        jnp.broadcast_to(array[None], (length, *array.shape)), axis, 0, 0, tiled=True
    )


def laid_out(tiles, dim):
    tiles = jnp.moveaxis(tiles, 0, dim)
    dims = tiles.shape
    return tiles.reshape(*dims[:dim], dims[dim] * dims[dim + 1], *dims[dim + 2 :])


def whole_of(array, axes, dim):
    far, near = axes
    first = from_everyone(array, far)
    tiles = jnp.swapaxes(from_everyone(first, near), 0, 1)
    return laid_out(tiles.reshape(-1, *array.shape), dim)


def rows_for(lines, length):
    spare = -len(lines) % length
    return jnp.pad(lines, [(0, spare)] + [(0, 0)] * (lines.ndim - 1))


def cut_along(array, dim, length):
    dims = array.shape
    tiles = array.reshape(*dims[:dim], length, dims[dim] // length, *dims[dim + 1 :])
    return jnp.moveaxis(tiles, dim, 0)


def sent_and_summed(array, axis, dim):
    length = lax.axis_size(axis)
    tiles = lax.all_to_all(cut_along(array, dim, length), axis, 0, 0, tiled=True)
    return jnp.sum(tiles, axis=0)


def sum_by_axis(array, axes, dim):
    far, near = axes
    tiles = cut_along(array, dim, lax.axis_size(far))
    nearer = sent_and_summed(tiles, near, dim + 1)
    arrived = lax.all_to_all(nearer, far, split_axis=0, concat_axis=0, tiled=True)
    return arrived.sum(axis=0)


def sum_by_parts(array, axes):
    lines = array.reshape(-1, array.shape[-1])
    padded = rows_for(lines, lax.axis_size(axes[0]) * lax.axis_size(axes[1]))
    whole = whole_of(sum_by_axis(padded, axes, 0), axes, 0)
    return lax.slice_in_dim(whole, 0, len(lines)).reshape(array.shape)


def sector_mask(sector_sizes, row_ids, col_ids):
    block_ends = jnp.cumsum(sector_sizes)
    row_block = jnp.sum((row_ids[:, None] >= block_ends[None, :]).astype(jnp.int32), axis=1)
    col_block = jnp.sum((col_ids[:, None] >= block_ends[None, :]).astype(jnp.int32), axis=1)
    return (jnp.abs(row_block[:, None] - col_block[None, :]) <= 2).astype(jnp.float32)


def mix_rows(mixing, operands):
    flat = operands.reshape(operands.shape[0], -1)
    mixed = jnp.dot(mixing, flat, preferred_element_type=jnp.float32).astype(jnp.bfloat16)
    return mixed.reshape(operands.shape)


def contract_joined(left, right):
    return lax.dot_general(
        left, right, (((1,), (1,)), ((), ())), preferred_element_type=jnp.float32
    )


def local(site_basis, left_ops, right_ops, integrals, wavefunction, pair_order, sector_sizes):
    row_count = wavefunction.shape[0]
    states = wavefunction.shape[1]
    pair_local = left_ops.shape[0]
    pair_total = integrals.shape[0]
    full_basis = whole_of(site_basis, (("wide_0", "wide_1", "narrow_0"), "narrow_1"), 0)
    rotated = jnp.dot(
        left_ops.reshape(pair_local * states, states),
        full_basis,
        preferred_element_type=jnp.float32,
    ).astype(jnp.bfloat16)
    side_by_side = (
        rotated.reshape(pair_local, states, states)
        .transpose(1, 0, 2)
        .reshape(states, pair_local * states)
    )
    built_wide = jnp.dot(full_basis.T, side_by_side, preferred_element_type=jnp.float32).astype(
        jnp.bfloat16
    )
    built_ops = built_wide.reshape(states, pair_local, states).transpose(1, 0, 2)
    built_rows = built_ops.reshape(pair_local * states, states)
    mixing = jnp.take(jnp.take(integrals, pair_order, axis=0), pair_order, axis=1)
    mixed_ops = mix_rows(
        mixing, lax.all_to_all(right_ops, WIDE_NARROW, split_axis=1, concat_axis=0, tiled=True)
    )
    comp_ops = lax.all_to_all(mixed_ops, WIDE_NARROW, split_axis=0, concat_axis=1, tiled=True)
    comp_joined = comp_ops.transpose(1, 0, 2).reshape(states, pair_local * states)
    first_row = lax.axis_index(WIDE_NARROW) * row_count
    row_ids = first_row + jnp.arange(row_count, dtype=jnp.int32)
    col_ids = jnp.arange(states, dtype=jnp.int32)
    local_mask = sector_mask(sector_sizes, row_ids, col_ids)
    local_state = (wavefunction.astype(jnp.float32) * local_mask).astype(jnp.bfloat16)
    summed = local_state.astype(jnp.float32)
    full_state = whole_of(local_state, (("wide_0", "wide_1", "narrow_0"), "narrow_1"), 0)
    step_size = 2.0 / math.sqrt(pair_total)
    full_mask = sector_mask(sector_sizes, col_ids, col_ids)
    for order_index in range(1, ORDER + 1):
        applied = jnp.dot(built_rows, full_state, preferred_element_type=jnp.float32).astype(
            jnp.bfloat16
        )
        applied_joined = (
            applied.reshape(pair_local, states, states)
            .transpose(1, 0, 2)
            .reshape(states, pair_local * states)
        )
        factor = -(step_size / order_index)
        partial_term = contract_joined(applied_joined, comp_joined)
        full_term = sum_by_parts(partial_term, (("wide_0", "wide_1", "narrow_0"), "narrow_1"))
        full_state = (factor * full_mask * full_term).astype(jnp.bfloat16)
        own_rows = lax.dynamic_slice_in_dim(full_state, first_row, row_count, 0)
        summed = summed + own_rows.astype(jnp.float32)
    return summed


def solution(mesh):
    torus = Mesh(mesh.devices.reshape(4, 2, 4, 4), ("wide_0", "wide_1", "narrow_0", "narrow_1"))
    in_specs = (
        P(WIDE_NARROW, None),
        P(WIDE_NARROW, None, None),
        P(WIDE_NARROW, None, None),
        P(),
        P(WIDE_NARROW, None),
        P(),
        P(),
    )
    out_specs = P(WIDE_NARROW, None)
    return jax.shard_map(local, mesh=torus, in_specs=in_specs, out_specs=out_specs, check_vma=False)
```

profile of v0, /device:TPU:1, one launch (start us, length us, event | category | flops | bytes accessed | tf_op | source)
XLA Modules:
  0.0 352.7 jit_solution(14016464976864734052)
XLA Ops:
  2.0 16.0 %all_to_all.113 = bf16[32,4,512]{2,1,0:T(4,128)(2,1)S(1)} all-to-all(bf16[32,4,512]{2,1,0:T(4,128)(2,1)S(1)} %broadcast_in_dim.42), channel_id=1, replica_groups=mesh['wide_0'=4,'wide_1'=2,'narrow_0'=4,'narrow_1'=4] {'wide_0','wide_1'..., dimensions={0} | all-to-all | bytes 262144 | tf_op jit(solution)/shard_map/all_to_all | solution.py:15
  18.7 11.4 %all_to_all.114 = bf16[32,4,512]{2,1,0:T(4,128)(2,1)S(1)} all-to-all(bf16[32,4,512]{2,1,0:T(4,128)(2,1)S(1)} %broadcast_in_dim.40), channel_id=1, replica_groups=mesh['wide_0'=4,'wide_1'=2,'narrow_0'=4,'narrow_1'=4] {'wide_0','wide_1'..., dimensions={0} | all-to-all | bytes 262144 | tf_op jit(solution)/shard_map/all_to_all | solution.py:15
  31.1 5.0 %all-to-all-start.3 = ((bf16[4,32,4,512]{3,2,1,0:T(4,128)(2,1)}), bf16[4,32,4,512]{3,2,1,0:T(4,128)(2,1)S(1)}, u32[]{:S(2)}, u32[]{:S(2)}) async-start(bf16[4,32,4,512]{3,2,1,0:T(4,128)(2,1)} %broadcast_in_dim.43), calls=%async_computation.3 | async-start | bytes 1048576 | tf_op jit(solution)/shard_map/all_to_all | solution.py:15
  36.1 4.0 %copy.129 = bf16[3,512,512]{2,0,1:T(4,128)(2,1)} copy(bf16[3,512,512]{2,1,0:T(8,128)(2,1)} %param.9) | data formatting | bytes 3145728 | tf_op args[2]
  40.2 4.9 %all-to-all-done.3 = bf16[4,32,4,512]{3,2,1,0:T(4,128)(2,1)S(1)} async-done(((bf16[4,32,4,512]{3,2,1,0:T(4,128)(2,1)}), bf16[4,32,4,512]{3,2,1,0:T(4,128)(2,1)S(1)}, u32[]{:S(2)}, u32[]{:S(2)}) %all-to-all-start.3) | async-done | bytes 524320 | tf_op jit(solution)/shard_map/all_to_all | solution.py:15
  45.1 5.9 %all-to-all-start.4 = ((bf16[3,512,512]{2,0,1:T(4,128)(2,1)}), bf16[3,512,512]{2,0,1:T(4,128)(2,1)}, u32[]{:S(2)}, u32[]{:S(2)}) async-start(bf16[3,512,512]{2,0,1:T(4,128)(2,1)} %copy.129), calls=%async_computation.4 | async-start | bytes 4194304 | tf_op jit(solution)/shard_map/all_to_all | solution.py:107
  53.3 27.2 %all-to-all-done.4 = bf16[3,512,512]{2,0,1:T(4,128)(2,1)} async-done(((bf16[3,512,512]{2,0,1:T(4,128)(2,1)}), bf16[3,512,512]{2,0,1:T(4,128)(2,1)}, u32[]{:S(2)}, u32[]{:S(2)}) %all-to-all-start.4) | async-done | bytes 1572896 | tf_op jit(solution)/shard_map/all_to_all | solution.py:107
  92.4 3.9 %reshape.116 = bf16[384,4,512]{2,1,0:T(4,128)(2,1)} reshape(bf16[384,2048]{1,0:T(8,128)(2,1)} %convolution_convert_fusion.5) | data formatting | bytes 3145728 | tf_op jit(solution)/shard_map/reshape | solution.py:75
  96.2 7.5 %all-to-all-start.5 = ((bf16[384,4,512]{2,1,0:T(4,128)(2,1)}), bf16[384,4,512]{2,1,0:T(4,128)(2,1)}, u32[]{:S(2)}, u32[]{:S(2)}) async-start(bf16[384,4,512]{2,1,0:T(4,128)(2,1)} %reshape.116), calls=%async_computation.5 | async-start | bytes 3145728 | tf_op jit(solution)/shard_map/all_to_all | solution.py:109
  118.3 9.2 %all-to-all-done.5 = bf16[384,4,512]{2,1,0:T(4,128)(2,1)} async-done(((bf16[384,4,512]{2,1,0:T(4,128)(2,1)}), bf16[384,4,512]{2,1,0:T(4,128)(2,1)}, u32[]{:S(2)}, u32[]{:S(2)}) %all-to-all-start.5) | async-done | bytes 1572896 | tf_op jit(solution)/shard_map/all_to_all | solution.py:109
  133.9 17.0 %all_to_all.115 = f32[4,32,4,512]{3,1,2,0:T(8,128)S(1)} all-to-all(f32[4,32,4,512]{3,1,2,0:T(8,128)S(1)} %fusion.6), channel_id=1, replica_groups=mesh['wide_0'=4,'wide_1'=2,'narrow_0'=4,'narrow_1'=4] {'narrow_1'}, dimensions={0} | all-to-all | bytes 2097152 | tf_op jit(solution)/shard_map/all_to_all | solution.py:46
  151.2 14.6 %all_to_all.116 = f32[32,4,512]{2,1,0:T(4,128)S(1)} all-to-all(f32[32,4,512]{2,1,0:T(4,128)S(1)} %copy.135), channel_id=1, replica_groups=mesh['wide_0'=4,'wide_1'=2,'narrow_0'=4,'narrow_1'=4] {'wide_0','wide_1'..., dimensions={0} | all-to-all | bytes 524288 | tf_op jit(solution)/shard_map/all_to_all | solution.py:54
  165.9 12.8 %all_to_all.117 = f32[32,4,512]{2,1,0:T(4,128)S(1)} all-to-all(f32[32,4,512]{2,1,0:T(4,128)S(1)} %broadcast_in_dim.48), channel_id=1, replica_groups=mesh['wide_0'=4,'wide_1'=2,'narrow_0'=4,'narrow_1'=4] {'wide_0','wide_1'..., dimensions={0} | all-to-all | bytes 524288 | tf_op jit(solution)/shard_map/all_to_all | solution.py:15
  179.8 3.7 %all-to-all-start.9 = ((f32[4,32,4,512]{3,2,1,0:T(4,128)}), f32[4,32,4,512]{3,2,1,0:T(4,128)S(1)}, u32[]{:S(2)}, u32[]{:S(2)}) async-start(f32[4,32,4,512]{3,2,1,0:T(4,128)} %broadcast_in_dim.49), calls=%async_computation.9 | async-start | bytes 2097152 | tf_op jit(solution)/shard_map/all_to_all | solution.py:15
  183.7 14.5 %all-to-all-done.9 = f32[4,32,4,512]{3,2,1,0:T(4,128)S(1)} async-done(((f32[4,32,4,512]{3,2,1,0:T(4,128)}), f32[4,32,4,512]{3,2,1,0:T(4,128)S(1)}, u32[]{:S(2)}, u32[]{:S(2)}) %all-to-all-start.9) | async-done | bytes 1048608 | tf_op jit(solution)/shard_map/all_to_all | solution.py:15
  209.3 16.5 %all_to_all.118 = f32[4,32,4,512]{3,1,2,0:T(8,128)S(1)} all-to-all(f32[4,32,4,512]{3,1,2,0:T(8,128)S(1)} %fusion.9), channel_id=1, replica_groups=mesh['wide_0'=4,'wide_1'=2,'narrow_0'=4,'narrow_1'=4] {'narrow_1'}, dimensions={0} | all-to-all | bytes 2097152 | tf_op jit(solution)/shard_map/all_to_all | solution.py:46
  226.1 14.0 %all_to_all.119 = f32[32,4,512]{2,1,0:T(4,128)S(1)} all-to-all(f32[32,4,512]{2,1,0:T(4,128)S(1)} %copy.142), channel_id=1, replica_groups=mesh['wide_0'=4,'wide_1'=2,'narrow_0'=4,'narrow_1'=4] {'wide_0','wide_1'..., dimensions={0} | all-to-all | bytes 524288 | tf_op jit(solution)/shard_map/all_to_all | solution.py:54
  240.2 12.8 %all_to_all.120 = f32[32,4,512]{2,1,0:T(4,128)S(1)} all-to-all(f32[32,4,512]{2,1,0:T(4,128)S(1)} %broadcast_in_dim.50), channel_id=1, replica_groups=mesh['wide_0'=4,'wide_1'=2,'narrow_0'=4,'narrow_1'=4] {'wide_0','wide_1'..., dimensions={0} | all-to-all | bytes 524288 | tf_op jit(solution)/shard_map/all_to_all | solution.py:15
  253.2 17.4 %all_to_all.121 = f32[4,32,4,512]{3,2,1,0:T(4,128)S(1)} all-to-all(f32[4,32,4,512]{3,2,1,0:T(4,128)S(1)} %broadcast_in_dim.51), channel_id=1, replica_groups=mesh['wide_0'=4,'wide_1'=2,'narrow_0'=4,'narrow_1'=4] {'narrow_1'}, dimensions={0} | all-to-all | bytes 2097152 | tf_op jit(solution)/shard_map/all_to_all | solution.py:15
  276.6 5.6 %dot_general.43 = bf16[32,4,4,1536]{3,2,1,0:T(4,128)(2,1)} reshape(bf16[512,3,512]{2,1,0:T(4,128)(2,1)} %bitcast.71) | data formatting | bytes 3145728 | tf_op jit(solution)/shard_map/dot_general | solution.py:79
  285.2 16.5 %all_to_all.122 = f32[4,32,4,512]{3,1,2,0:T(8,128)S(1)} all-to-all(f32[4,32,4,512]{3,1,2,0:T(8,128)S(1)} %fusion.12), channel_id=1, replica_groups=mesh['wide_0'=4,'wide_1'=2,'narrow_0'=4,'narrow_1'=4] {'narrow_1'}, dimensions={0} | all-to-all | bytes 2097152 | tf_op jit(solution)/shard_map/all_to_all | solution.py:46
  302.0 14.0 %all_to_all.123 = f32[32,4,512]{2,1,0:T(4,128)S(1)} all-to-all(f32[32,4,512]{2,1,0:T(4,128)S(1)} %copy.148), channel_id=1, replica_groups=mesh['wide_0'=4,'wide_1'=2,'narrow_0'=4,'narrow_1'=4] {'wide_0','wide_1'..., dimensions={0} | all-to-all | bytes 524288 | tf_op jit(solution)/shard_map/all_to_all | solution.py:54
  316.1 12.8 %all_to_all.124 = f32[32,4,512]{2,1,0:T(4,128)S(1)} all-to-all(f32[32,4,512]{2,1,0:T(4,128)S(1)} %broadcast_in_dim.52), channel_id=1, replica_groups=mesh['wide_0'=4,'wide_1'=2,'narrow_0'=4,'narrow_1'=4] {'wide_0','wide_1'..., dimensions={0} | all-to-all | bytes 524288 | tf_op jit(solution)/shard_map/all_to_all | solution.py:15
  339.2 9.3 %all-to-all-done.17 = f32[4,32,4,512]{3,2,1,0:T(4,128)S(1)} async-done(((f32[4,32,4,512]{3,2,1,0:T(4,128)}), f32[4,32,4,512]{3,2,1,0:T(4,128)S(1)}, u32[]{:S(2)}, u32[]{:S(2)}) %all-to-all-start.17) | async-done | bytes 1048608 | tf_op jit(solution)/shard_map/all_to_all | solution.py:15
  (91 shorter events, 75.6 us)
Async XLA Ops:
  0.0 106.1 %copy-start = (bf16[3,512,512]{2,1,0:T(8,128)(2,1)S(1)}, bf16[3,512,512]{2,1,0:T(8,128)(2,1)}, u32[]{:S(2)}) copy-start(bf16[3,512,512]{2,1,0:T(8,128)(2,1)} %param.8) | copy-start | bytes 4718596
  31.1 14.0 %all-to-all-start.3 = ((bf16[4,32,4,512]{3,2,1,0:T(4,128)(2,1)}), bf16[4,32,4,512]{3,2,1,0:T(4,128)(2,1)S(1)}, u32[]{:S(2)}, u32[]{:S(2)}) async-start(bf16[4,32,4,512]{3,2,1,0:T(4,128)(2,1)} %broadcast_in_dim.43), calls=%async_computation.3 | async-start | bytes 1048576 | tf_op jit(solution)/shard_map/all_to_all | solution.py:15
  40.2 10.9 %copy-start.7 = (s32[384]{0:T(512)S(1)}, s32[384]{0:T(512)}, u32[]{:S(2)}) copy-start(s32[384]{0:T(512)} %param.12) | copy-start | bytes 4612
  40.2 10.9 %copy-start.2 = (bf16[384,384]{1,0:T(8,128)(2,1)S(1)}, bf16[384,384]{1,0:T(8,128)(2,1)}, u32[]{:S(2)}) copy-start(bf16[384,384]{1,0:T(8,128)(2,1)} %param.10) | copy-start | bytes 884740
  45.1 35.3 %all-to-all-start.4 = ((bf16[3,512,512]{2,0,1:T(4,128)(2,1)}), bf16[3,512,512]{2,0,1:T(4,128)(2,1)}, u32[]{:S(2)}, u32[]{:S(2)}) async-start(bf16[3,512,512]{2,0,1:T(4,128)(2,1)} %copy.129), calls=%async_computation.4 | async-start | bytes 4194304 | tf_op jit(solution)/shard_map/all_to_all | solution.py:107
  81.4 14.8 %all-to-all-start.1 = ((bf16[4,32,4,512]{3,2,1,0:T(4,128)(2,1)}), bf16[4,32,4,512]{3,2,1,0:T(4,128)(2,1)S(1)}, u32[]{:S(2)}, u32[]{:S(2)}) async-start(bf16[4,32,4,512]{3,2,1,0:T(4,128)(2,1)} %broadcast_in_dim.41), calls=%async_computation.1 | async-start | bytes 1048576 | tf_op jit(solution)/shard_map/all_to_all | solution.py:15
  96.2 31.3 %all-to-all-start.5 = ((bf16[384,4,512]{2,1,0:T(4,128)(2,1)}), bf16[384,4,512]{2,1,0:T(4,128)(2,1)}, u32[]{:S(2)}, u32[]{:S(2)}) async-start(bf16[384,4,512]{2,1,0:T(4,128)(2,1)} %reshape.116), calls=%async_computation.5 | async-start | bytes 3145728 | tf_op jit(solution)/shard_map/all_to_all | solution.py:109
  111.6 2.4 copy-start.4
  129.9 1.6 copy-start.3
  179.8 18.4 %all-to-all-start.9 = ((f32[4,32,4,512]{3,2,1,0:T(4,128)}), f32[4,32,4,512]{3,2,1,0:T(4,128)S(1)}, u32[]{:S(2)}, u32[]{:S(2)}) async-start(f32[4,32,4,512]{3,2,1,0:T(4,128)} %broadcast_in_dim.49), calls=%async_computation.9 | async-start | bytes 2097152 | tf_op jit(solution)/shard_map/all_to_all | solution.py:15
  183.7 16.4 %copy-start.5 = (bf16[512,3,512]{2,0,1:T(8,128)(2,1)S(1)}, bf16[512,3,512]{2,0,1:T(8,128)(2,1)}, u32[]{:S(2)}) copy-start(bf16[512,3,512]{2,0,1:T(8,128)(2,1)} %copy-done.4) | copy-start | bytes 4718596
  330.1 18.4 %all-to-all-start.17 = ((f32[4,32,4,512]{3,2,1,0:T(4,128)}), f32[4,32,4,512]{3,2,1,0:T(4,128)S(1)}, u32[]{:S(2)}, u32[]{:S(2)}) async-start(f32[4,32,4,512]{3,2,1,0:T(4,128)} %broadcast_in_dim.53), calls=%async_computation.17 | async-start | bytes 2097152 | tf_op jit(solution)/shard_map/all_to_all | solution.py:15
  348.5 4.2 %copy-start.1 = (bf16[3,512,512]{2,1,0:T(8,128)(2,1)S(1)}, bf16[3,512,512]{2,1,0:T(8,128)(2,1)}, u32[]{:S(2)}) copy-start(bf16[3,512,512]{2,1,0:T(8,128)(2,1)} %param.8) | copy-start | bytes 4718596
  349.6 1.6 copy-start.6
where the time goes:
time: 354 us; the launch traced here: 353 us
  blocking collectives  176 us (50%)
  waiting for transfers between devices  65.2 us (18%)
  local copies, waits for them, and re-layouts  55.1 us (16%)
  starting transfers between devices  29.2 us (8%)
  matrix products  21.4 us (6%)
  other arithmetic  5.55 us (2%)
    all_to_all x6, blocking collectives, from_everyone(): lax.all_to_all(jnp.broadcast_to(array[None], (length, *array.shape)), axi...  83.2 us
    all_to_all x3, blocking collectives, sent_and_summed(): lax.all_to_all(cut_along(array, dim, length), axis, 0, 0, tiled=True)  50 us
    all_to_all x3, blocking collectives, sum_by_axis(): lax.all_to_all(nearer, far, split_axis=0, concat_axis=0, tiled=True)  42.6 us
    all_to_all x4, waiting for transfers between devices, from_everyone(): lax.all_to_all(jnp.broadcast_to(array[None], (length, *array.shape)), axi...  28.8 us
    all_to_all x1, waiting for transfers between devices, local(): lax.all_to_all(right_ops, WIDE_NARROW, split_axis=1, concat_axis=0, tiled...  27.2 us
    all_to_all x4, starting transfers between devices, from_everyone(): lax.all_to_all(jnp.broadcast_to(array[None], (length, *array.shape)), axi...  15.7 us
    dot_general x3, local copies, waits for them, and re-layouts, contract_joined(): lax.dot_general(left, right, (((1,), (1,)), ((), ())), preferred_element_...  11.4 us
    all_to_all x1, waiting for transfers between devices, local(): lax.all_to_all(mixed_ops, WIDE_NARROW, split_axis=0, concat_axis=1, tiled...  9.21 us
  transfers between devices with their start and end apart: 6, of which 5 were waited for; matrix products, arithmetic and copies ran while one was open for 11% of the time, Pallas kernels for 0%

commit v1 on v0

v1 whole, which is shorter than its diff:
```python
import math

import jax
import jax.numpy as jnp
from jax import lax
from jax.experimental import pallas as pl
from jax.experimental.pallas import tpu as pltpu
from jax.sharding import PartitionSpec as P

ORDER = 3
ROWS, LANES = 16, 128
BF16, F32 = jnp.bfloat16, jnp.float32
BOTH = ("wide", "narrow")
MESH = pl.DeviceIdType.MESH


def dot(a, b, dims=((1,), (0,))):
    return lax.dot_general(a, b, (dims, ((), ())), preferred_element_type=F32)


def iota(shape, dim):
    return lax.broadcasted_iota(jnp.int32, shape, dim)


def tile_swap(size):
    o, m = iota((size, size), 0), iota((size, size), 1)
    return (m == (o & 15) * 16 + (o >> 4)).astype(F32).astype(BF16)


def row_blocks(o):
    return ((o & 63) >> 2) * 16 + (o >> 6) * 4 + (o & 3)


def kernel(
    order_ref, sizes_ref, basis_ref, left_ref, right_ref, integrals_ref, wave_ref,
    out_ref,
    left_v, pack_v, bw_v, u_v, built_v, applied_v, recv_v, bm_v, ym_v, cbuf_v, comp_v,
    mix_v, state_v, part_v, rs_v, last_v, tile_v, local_sem, send_sem, recv_sem,
    *, states, pairs, parts,
):
    per = pairs // parts
    wide, narrow = lax.axis_size("wide"), lax.axis_size("narrow")
    w, n = lax.axis_index("wide"), lax.axis_index("narrow")
    me = w * narrow + n
    across = states // LANES
    step_size = 2.0 / math.sqrt(pairs)

    def peer(k):
        p = lax.rem(me + k, parts)
        return p, (p // narrow, lax.rem(p, narrow))

    def tile_of(p):
        return (
            pl.ds(pl.multiple_of(p // across * ROWS, ROWS), ROWS),
            pl.ds(pl.multiple_of(lax.rem(p, across) * LANES, LANES), LANES),
        )

    def send_all(phase, src, dst):
        def step(k, carry):
            p, device = peer(k)
            pltpu.make_async_remote_copy(
                src_ref=src(p), dst_ref=dst, send_sem=send_sem.at[phase],
                recv_sem=recv_sem.at[phase], device_id=device, device_id_type=MESH,
            ).start()
            return carry

        lax.fori_loop(1, parts, step, 0)

    def wait_bytes(sem, phase, ref):
        pltpu.make_async_copy(ref, ref, sem.at[phase]).wait()

    barrier = pltpu.get_barrier_semaphore()

    def greet(k, carry):
        _, device = peer(k)
        pl.semaphore_signal(barrier, inc=1, device_id=device, device_id_type=MESH)
        return carry

    lax.fori_loop(1, parts, greet, 0)
    left_copy = pltpu.make_async_copy(left_ref, left_v, local_sem.at[0])
    left_copy.start()
    mine = pl.ds(me * per, per)
    mine_rows, mine_cols = tile_of(me)
    own_copy = pltpu.make_async_copy(
        right_ref.at[:, mine_rows, mine_cols], recv_v.at[mine], local_sem.at[1]
    )
    own_copy.start()

    def packed(ref):
        rows = ref[...].astype(F32)
        return jnp.concatenate(
            [rows[:, c * LANES : (c + 1) * LANES] for c in range(across)], axis=0
        ).astype(BF16)

    pack_v[0] = packed(basis_ref)
    pack_v[1] = packed(wave_ref)
    bw_v[me] = pack_v[...]

    chosen = (iota((pairs, pairs), 0) == order_ref[...]).astype(F32).astype(BF16)
    by_column = dot(integrals_ref[...], chosen).astype(BF16)
    mix_v[...] = dot(chosen, by_column, ((0,), (0,))).astype(BF16)

    ends, total = [], jnp.int32(0)
    for b in range(sizes_ref.shape[0]):
        total = total + sizes_ref[b]
        ends.append(total)

    def block_of(ids):
        found = jnp.zeros_like(ids)
        for end in ends:
            found = found + (ids >= end).astype(jnp.int32)
        return found

    def mask_of(row_ids, col_ids):
        return (jnp.abs(block_of(row_ids) - block_of(col_ids)) <= 2).astype(F32)

    pl.semaphore_wait(barrier, parts - 1)
    send_all(0, lambda p: pack_v, bw_v.at[me])
    send_all(1, lambda p: right_ref.at[(slice(None), *tile_of(p))], recv_v.at[mine])

    wait_bytes(recv_sem, 0, bw_v.at[pl.ds(0, parts - 1)])
    square = (256, 256)
    spread = (iota(square, 1) == row_blocks(iota(square, 0))).astype(F32).astype(BF16)
    gather = (iota(square, 0) == row_blocks(iota(square, 1))).astype(F32).astype(BF16)
    for g in range(states // 64):
        both = jnp.concatenate(
            [bw_v[16 * g : 16 * (g + 1), i].reshape(256, LANES) for i in range(2)], axis=1
        )
        both = dot(spread, both)
        for c in range(across):
            rows, cols = slice(64 * g, 64 * (g + 1)), slice(c * LANES, (c + 1) * LANES)
            mask = mask_of(
                64 * g + iota((64, 1), 0), c * LANES + iota((1, LANES), 1)
            )
            block = both[64 * c : 64 * (c + 1)]
            u_v[rows, cols] = block[:, :LANES].astype(BF16)
            state_v[0, rows, cols] = (block[:, LANES:] * mask).astype(BF16)

    left_copy.wait()

    def build(s, carry):
        rotated = dot(left_v[s], u_v[...]).astype(BF16)
        built_v[s] = dot(u_v[...], rotated, ((0,), (0,))).astype(BF16)
        return carry

    lax.fori_loop(0, per, build, 0)

    def apply(k):
        def one(s, carry):
            applied_v[s] = dot(built_v[s], state_v[k]).astype(BF16)
            return carry

        lax.fori_loop(0, per, one, 0)

    apply(0)

    own_copy.wait()
    wait_bytes(recv_sem, 1, recv_v.at[pl.ds(0, pairs - per)])
    swap = tile_swap(256)

    def into_rows(q, carry):
        base = pl.multiple_of(q * 32, 32)
        both = jnp.concatenate(
            [recv_v[pl.ds(base + 16 * i, 16)].reshape(256, LANES) for i in range(2)], axis=1
        )
        both = dot(swap, both).astype(BF16)
        for r in range(16):
            for i in range(2):
                bm_v[pl.ds(base + 16 * i, 16), r * LANES : (r + 1) * LANES] = both[
                    16 * r : 16 * (r + 1), i * LANES : (i + 1) * LANES
                ]
        return carry

    lax.fori_loop(0, pairs // 32, into_rows, 0)

    def mix(c, carry):
        cols = pl.ds(pl.multiple_of(c * 256, 256), 256)
        ym_v[:, cols] = dot(mix_v[...], bm_v[:, cols]).astype(BF16)
        return carry

    lax.fori_loop(0, 8, mix, 0)

    def into_tiles(q, carry):
        base = pl.multiple_of(q * 32, 32)
        both = jnp.concatenate(
            [
                jnp.concatenate(
                    [
                        ym_v[pl.ds(base + 16 * i, 16), r * LANES : (r + 1) * LANES]
                        for r in range(16)
                    ],
                    axis=0,
                )
                for i in range(2)
            ],
            axis=1,
        )
        both = dot(swap, both).astype(BF16)
        for i in range(2):
            cbuf_v[pl.ds(base + 16 * i, 16)] = both[:, i * LANES : (i + 1) * LANES].reshape(
                16, 16, LANES
            )
        return carry

    lax.fori_loop(0, pairs // 32, into_tiles, 0)
    send_all(2, lambda p: cbuf_v.at[pl.ds(p * per, per)], comp_v.at[:, mine_rows, mine_cols])
    comp_v[:, mine_rows, mine_cols] = cbuf_v[mine]
    wait_bytes(recv_sem, 2, cbuf_v.at[pl.ds(0, pairs - per)])

    def term():
        def one(i, carry):
            rows = pl.ds(pl.multiple_of(i * 256, 256), 256)
            total = dot(applied_v[0, rows, :], comp_v[0], ((1,), (1,)))
            for s in range(1, per):
                total += dot(applied_v[s, rows, :], comp_v[s], ((1,), (1,)))
            part_v[rows, :] = total.astype(BF16)
            return carry

        lax.fori_loop(0, states // 256, one, 0)

    def summed(slot):
        def some(j, carry):
            return carry + jnp.sum(rs_v[slot, pl.ds(j * 8, 8)].astype(F32), axis=0)

        return lax.fori_loop(0, parts // 8, some, jnp.zeros((ROWS, LANES), F32))

    tiles = parts - 1
    for k in range(1, ORDER):
        term()
        slot = k - 1
        send_all(1 + 2 * k, lambda p: part_v.at[tile_of(p)], rs_v.at[slot, me])
        rs_v[slot, me] = part_v[mine_rows, mine_cols]
        mask = mask_of(
            me // across * ROWS + iota((ROWS, 1), 0),
            lax.rem(me, across) * LANES + iota((1, LANES), 1),
        )
        factor = -(step_size / k)
        wait_bytes(recv_sem, 1 + 2 * k, rs_v.at[slot, pl.ds(0, tiles)])
        new = (factor * mask * summed(slot)).astype(BF16)
        tile_v[slot] = new
        state_v[k, mine_rows, mine_cols] = new
        send_all(2 + 2 * k, lambda p: tile_v.at[slot], state_v.at[(k, mine_rows, mine_cols)])
        wait_bytes(send_sem, 1 + 2 * k, rs_v.at[slot, pl.ds(0, tiles)])
        wait_bytes(recv_sem, 2 + 2 * k, rs_v.at[slot, pl.ds(0, tiles)])
        apply(k)

    term()
    for g in range(states // 64):
        stacked = jnp.concatenate(
            [
                part_v[64 * g : 64 * (g + 1), c * LANES : (c + 1) * LANES]
                for c in range(across)
            ],
            axis=0,
        )
        last_v[16 * g : 16 * (g + 1)] = dot(gather, stacked).astype(BF16).reshape(16, 16, LANES)
    slot, phase = ORDER - 1, 1 + 2 * ORDER
    send_all(phase, lambda p: last_v.at[p], rs_v.at[slot, me])
    rs_v[slot, me] = last_v[me]
    own_rows = states // parts
    pick = (iota((8, states), 1) == own_rows * me + iota((8, states), 0)).astype(F32).astype(BF16)
    so_far = dot(pick, state_v[0])
    for k in range(1, ORDER):
        so_far += dot(pick, state_v[k])
    wait_bytes(recv_sem, phase, rs_v.at[slot, pl.ds(0, tiles)])
    total = summed(slot)
    for c in range(across):
        mask = mask_of(
            own_rows * me + iota((own_rows, 1), 0), c * LANES + iota((1, LANES), 1)
        )
        new = -(step_size / ORDER) * mask * total[own_rows * c : own_rows * (c + 1)]
        cols = slice(c * LANES, (c + 1) * LANES)
        out_ref[:, cols] = so_far[:own_rows, cols] + new.astype(BF16).astype(F32)

    wait_bytes(send_sem, 0, bw_v.at[pl.ds(0, tiles)])
    wait_bytes(send_sem, 1, recv_v.at[pl.ds(0, pairs - per)])
    wait_bytes(send_sem, 2, recv_v.at[pl.ds(0, pairs - per)])
    for k in range(1, ORDER):
        wait_bytes(send_sem, 2 + 2 * k, rs_v.at[slot, pl.ds(0, tiles)])
    wait_bytes(send_sem, phase, rs_v.at[slot, pl.ds(0, tiles)])


def local(site_basis, left_ops, right_ops, integrals, wavefunction, pair_order, sector_sizes):
    states = wavefunction.shape[1]
    pairs = integrals.shape[0]
    per = left_ops.shape[0]
    parts = pairs // per
    vmem = pl.BlockSpec(memory_space=pltpu.VMEM)
    anywhere = pl.BlockSpec(memory_space=pl.ANY)
    ops = (per, states, states)
    phases = 2 + 2 * ORDER
    body = lambda *refs: kernel(*refs, states=states, pairs=pairs, parts=parts)
    return pl.pallas_call(
        body,
        out_shape=jax.ShapeDtypeStruct(wavefunction.shape, F32),
        in_specs=[
            vmem, pl.BlockSpec(memory_space=pltpu.SMEM), vmem, anywhere, anywhere, vmem, vmem
        ],
        out_specs=vmem,
        scratch_shapes=[
            pltpu.VMEM(ops, BF16),
            pltpu.VMEM((2, ROWS, LANES), BF16),
            pltpu.VMEM((parts, 2, ROWS, LANES), BF16),
            pltpu.VMEM((states, states), BF16),
            pltpu.VMEM(ops, BF16),
            pltpu.VMEM(ops, BF16),
            pltpu.VMEM((pairs, ROWS, LANES), BF16),
            pltpu.VMEM((pairs, ROWS * LANES), BF16),
            pltpu.VMEM((pairs, ROWS * LANES), BF16),
            pltpu.VMEM((pairs, ROWS, LANES), BF16),
            pltpu.VMEM(ops, BF16),
            pltpu.VMEM((pairs, pairs), BF16),
            pltpu.VMEM((ORDER, states, states), BF16),
            pltpu.VMEM((states, states), BF16),
            pltpu.VMEM((ORDER, parts, ROWS, LANES), BF16),
            pltpu.VMEM((parts, ROWS, LANES), BF16),
            pltpu.VMEM((ORDER, ROWS, LANES), BF16),
            pltpu.SemaphoreType.DMA((2,)),
            pltpu.SemaphoreType.DMA((phases,)),
            pltpu.SemaphoreType.DMA((phases,)),
        ],
        compiler_params=pltpu.CompilerParams(
            collective_id=0, has_side_effects=True, vmem_limit_bytes=48 << 20
        ),
    )(
        pair_order.reshape(1, pairs), sector_sizes, site_basis, left_ops, right_ops,
        integrals, wavefunction,
    )


def solution(mesh):
    in_specs = (
        P(BOTH, None), P(BOTH, None, None), P(BOTH, None, None), P(), P(BOTH, None), P(), P()
    )
    return jax.shard_map(
        local, mesh=mesh, in_specs=in_specs, out_specs=P(BOTH, None), check_vma=False
    )
```

time: 354 us -> 142 us (0.40)
  blocking collectives: 176 us -> 0 us
  Pallas kernels: 0 us -> 135 us
  waiting for transfers between devices: 65.2 us -> 0 us
  local copies, waits for them, and re-layouts: 55.1 us -> 7.09 us
  starting transfers between devices: 29.2 us -> 0 us
  matrix products: 21.4 us -> 0 us
  other arithmetic: 5.55 us -> 0 us
    all_to_all x12 -> x0, blocking collectives: 176 us -> none  [the longest x6 83.2 us: from_everyone(): lax.all_to_all(jnp.broadcast_to(array[None], (length, *array.shape)), axi...]
    pallas_call x0 -> x1, Pallas kernels: none -> 135 us  [local(): pl.pallas_call(body, out_shape=jax.ShapeDtypeStruct(wavefunction.shape, F...]
    all_to_all x6 -> x0, waiting for transfers between devices: 65.2 us -> none  [the longest x4 28.8 us: from_everyone(): lax.all_to_all(jnp.broadcast_to(array[None], (length, *array.shape)), axi...]
    all_to_all x6 -> x0, starting transfers between devices: 29.2 us -> none  [the longest x4 15.7 us: from_everyone(): lax.all_to_all(jnp.broadcast_to(array[None], (length, *array.shape)), axi...]
    dot_general x9 -> x0, matrix products: 21.4 us -> none  [the longest x3 8.36 us: contract_joined(): lax.dot_general(left, right, (((1,), (1,)), ((), ())), preferred_element_...]
    dot_general x3 -> x0, local copies, waits for them, and re-layouts: 11.4 us -> none  [contract_joined(): lax.dot_general(left, right, (((1,), (1,)), ((), ())), preferred_element_...]
    reshape x6 -> x1, local copies, waits for them, and re-layouts: 10.7 us -> 0.68 us  [local(): pair_order.reshape(1, pairs)]
    another operation x5 -> x0, local copies, waits for them, and re-layouts: 7.44 us -> none  [laid_out(): tiles.reshape(*dims[:dim], dims[dim] * dims[dim + 1], *dims[dim + 2:])]
  transfers between devices with their start and end apart: 6 -> 0, of which waited for: 5 -> 0; matrix products, arithmetic and copies ran while one was open for 11% -> 0% of each run, Pallas kernels for 0% -> 0%
where the time goes in v1:
time: 142 us
  Pallas kernels  135 us (95%)
  local copies, waits for them, and re-layouts  7.09 us (5%)
    pallas_call x1, Pallas kernels, local(): pl.pallas_call(body, out_shape=jax.ShapeDtypeStruct(wavefunction.shape, F...  135 us
    unnamed x13, local copies, waits for them, and re-layouts  6.4 us

profile of v1, /device:TPU:1, one launch (start us, length us, event | category | flops | bytes accessed | tf_op | source)
XLA Modules:
  0.0 142.1 jit_solution(12549936865369962215)
XLA Ops:
  0.0 0.7 reshape.3.refs_0_
  0.7 0.0 copy-start
  0.7 1.4 copy-done
  2.1 0.0 copy-start.1
  2.1 1.4 copy-done.1
  3.5 0.0 copy-start.2
  3.5 1.0 copy-done.2
  4.5 0.0 copy-start.3
  4.5 0.7 copy-done.3
  5.2 0.0 copy-start.4
  5.2 0.7 copy-done.4
  5.8 0.0 copy-start.5
  5.8 0.7 copy-done.5
  6.5 135.0 %shard_map.73 = f32[4,512]{1,0:T(4,128)S(1)} custom-call(s32[1,384]{1,0:T(1,128)S(1)} %reshape.3.refs_0_, s32[8]{0:T(128)S(1)} %copy-done.5, bf16[4,512]{1,0:T(4,128)(2,1)S(1)} %copy-done.3, bf16[3,512,512]{2,1,0:T(8,128)(2,1)S(1)} %copy-done, bf16[3,512,512]{2,1,0:T(8,128)(2,1)S(1)} %copy-done.1, bf16[384,384]{1,0:T(8,128)(2,1)S(1)} %copy-done.2, ...), custom_call_target="tpu_custom_call" | custom-call | tf_op jit(solution)/shard_map/pallas_call | solution.py:293
  141.5 0.6 copy.9
Async XLA Ops:
  0.7 1.4 copy-start
  2.1 1.4 copy-start.1
  3.5 1.0 copy-start.2
  4.5 0.7 copy-start.3
  5.2 0.7 copy-start.4
  5.8 0.7 copy-start.5

commit v2 on v1

v2 whole, which is shorter than its diff:
```python
import math

import jax
import jax.numpy as jnp
from jax import lax
from jax.experimental import pallas as pl
from jax.experimental.pallas import tpu as pltpu
from jax.sharding import PartitionSpec as P

ORDER = 3
ROWS, LANES = 16, 128
BF16, F32 = jnp.bfloat16, jnp.float32
BOTH = ("wide", "narrow")
MESH = pl.DeviceIdType.MESH


def dot(a, b, dims=((1,), (0,))):
    return lax.dot_general(a, b, (dims, ((), ())), preferred_element_type=F32)


def iota(shape, dim):
    return lax.broadcasted_iota(jnp.int32, shape, dim)


def tile_swap(size):
    o, m = iota((size, size), 0), iota((size, size), 1)
    return (m == (o & 15) * 16 + (o >> 4)).astype(F32).astype(BF16)


def spread_row(o):
    return ((o & 63) >> 2) * 16 + (o >> 6) * 4 + (o & 3)


def gather_row(o):
    return ((o >> 2) & 1) * 128 + ((o >> 3) & 1) * 64 + (o >> 4) * 4 + (o & 3)


def far_first(depth):
    steps = [
        (dy, dx, dz) for dy in range(4) for dx in range(4) for dz in range(depth)
    ]
    hops = lambda d: min(d[0], 4 - d[0]) + min(d[1], 4 - d[1])
    along_z = lambda d: min(d[2], 4 - d[2]) if depth == 4 else 2 * d[2]
    return sorted(steps, key=lambda d: -hops(d) - along_z(d))


def kernel(
    order_ref, sizes_ref, basis_ref, left_ref, right_ref, integrals_ref, wave_ref,
    out_ref,
    order_v, sizes_v, basis_v, integrals_v, wave_v,
    left_v, pack_v, bw_v, u_v, built_v, applied_v, recv_v, bm_v, ym_v, cbuf_v, comp_v,
    mix_v, state_v, part_v, rs_v, last_v, tile_v, swap_v, pair_v, other_v, acc_v, local_sem, send_sem, recv_sem,
    *, states, pairs, parts,
):
    per = pairs // parts
    phases = 6 + 3 * ORDER
    group = 2 * per
    narrow = lax.axis_size("narrow")
    w, n = lax.axis_index("wide"), lax.axis_index("narrow")
    core = lax.rem(w, 2)
    me = w * narrow + n
    chips = parts // 2
    chip = w // 2 * narrow + n
    partner = (w + 1 - 2 * core, n)
    across = states // LANES
    half = states // 2
    step_size = 2.0 / math.sqrt(pairs)

    y, x, z = w // 2, n // 4, lax.rem(n, 4)

    to_w = [lax.rem(y + d, 4) * 2 + core for d in range(4)]
    to_y = [lax.rem(y + d, 4) * narrow for d in range(4)]
    to_x = [lax.rem(x + d, 4) * 4 for d in range(4)]
    to_z = [lax.rem(z + d, 4) for d in range(4)]

    def block(row, col):
        return (
            pl.ds(pl.multiple_of(row * ROWS, ROWS), ROWS),
            pl.ds(pl.multiple_of(col * LANES, LANES), LANES),
        )

    def mix_block(q):
        return block(lax.div(q, across), lax.rem(q, across))

    def term_block(q):
        return block(lax.rem(q, 2) * (chips // 4) + lax.div(q, 4), lax.div(lax.rem(q, 4), 2))

    def mix_slots(q):
        return pl.ds((lax.rem(q, 2) * (chips // 2) + lax.div(q, 2)) * group, group)

    def send(phase, src, dst, device):
        pltpu.make_async_remote_copy(
            src_ref=src, dst_ref=dst, send_sem=send_sem.at[phase],
            recv_sem=recv_sem.at[phase], device_id=device, device_id_type=MESH,
        ).start()

    def each_chip(visit):
        to_n = [[i + j for j in to_z] for i in to_x]
        for dy, dx, dz in far_first(4):
            if (dy, dx, dz) != (0, 0, 0):
                visit(to_y[dy] + to_n[dx][dz], (to_w[dy], to_n[dx][dz]))

    def send_chips(phase, src, dst):
        each_chip(lambda q, device: send(phase, src(q), dst, device))

    def send_half(phase, parity, src, dst):
        first = lax.rem(parity + z, 2)
        to_n = [[i + lax.rem(z + first + 2 * j, 4) for j in range(2)] for i in to_x]
        for dy, dx, dz in far_first(2):
            q, device = to_y[dy] + to_n[dx][dz], (to_w[dy], to_n[dx][dz])
            if (dy, dx, dz) == (0, 0, 0):

                @pl.when(first == 1)
                def _():
                    send(phase, src(q), dst, device)

            else:
                send(phase, src(q), dst, device)

    def wait_bytes(sem, phase, ref):
        pltpu.make_async_copy(ref, ref, sem.at[phase]).wait()

    barrier = pltpu.get_barrier_semaphore()

    def greet(device):
        pl.semaphore_signal(barrier, inc=1, device_id=device, device_id_type=MESH)

    greet(partner)
    each_chip(lambda q, device: greet(device))
    half_rows = half // ROWS
    own_half = pl.ds(pl.multiple_of(core * half, half), half)
    other_half = pl.ds(pl.multiple_of((1 - core) * half, half), half)
    own_slots = pl.ds(core * (pairs // 2) + chip * per, per)
    other_slots = pl.ds((1 - core) * (pairs // 2) + chip * per, per)
    mix_rows, mix_cols = mix_block(chip)
    term_rows, term_cols = term_block(chip)
    loads = [
        pltpu.make_async_copy(src, dst, local_sem.at[i])
        for i, (src, dst) in enumerate(
            [
                (order_ref, order_v), (sizes_ref, sizes_v), (integrals_ref, integrals_v),
                (basis_ref, basis_v), (wave_ref, wave_v),
                (right_ref.at[:, block(core * half_rows + chip // across, 0)[0], mix_cols],
                 recv_v.at[own_slots]),
                (left_ref, left_v.at[pl.ds(core * per, per)]),
            ]
        )
    ]
    for load in loads:
        load.start()
    for load in loads[:5]:
        load.wait()

    def packed(ref):
        rows = ref[...].astype(F32)
        return jnp.concatenate(
            [rows[:, c * LANES : (c + 1) * LANES] for c in range(across)], axis=0
        ).astype(BF16)

    pack_v[0] = packed(basis_v)
    pack_v[1] = packed(wave_v)
    bw_v[core, chip] = pack_v[...]
    swap_v[...] = tile_swap(256)

    def take(ids, width):
        return (iota((pairs, width), 0) == ids).astype(F32).astype(BF16)

    def slot(of_chip, of_core, j):
        return ((of_chip // narrow * 2 + of_core) * narrow + (of_chip & (narrow - 1))) * per + j

    chosen = take(order_v[...], pairs)
    place = iota((1, pairs), 1)
    owner = (place * (65536 // group + 1)) >> 16
    rest = place - owner * group
    of_core = (rest >= per).astype(jnp.int32)
    owner = (owner & (chips // 2 - 1)) * 2 + owner // (chips // 2)
    by_row = dot(chosen, take(slot(owner, of_core, rest - of_core * per), pairs)).astype(BF16)
    place = iota((1, pairs // 2), 1)
    sender = (place * (65536 // per + 1)) >> 16
    for c in range(2):
        by_column = dot(chosen, take(slot(sender, c, place - sender * per), pairs // 2))
        by_column = dot(integrals_v[...], by_column.astype(BF16)).astype(BF16)
        mix_v[c] = dot(by_row, by_column, ((0,), (0,))).astype(BF16)

    ends, total = [], jnp.int32(0)
    for b in range(sizes_ref.shape[0]):
        total = total + sizes_v[b]
        ends.append(total)

    def block_of(ids):
        found = jnp.zeros_like(ids)
        for end in ends:
            found = found + (ids >= end).astype(jnp.int32)
        return found

    def mask_of(row_ids, col_ids):
        return (jnp.abs(block_of(row_ids) - block_of(col_ids)) <= 2).astype(F32)

    pl.semaphore_wait(barrier, chips)

    send(phases - 1, right_ref.at[:, other_half, :], other_v, partner)
    send_chips(
        1,
        lambda q: right_ref.at[
            (slice(None), *block(core * half_rows + lax.div(q, across), lax.rem(q, across)))
        ],
        recv_v.at[own_slots],
    )
    wait_bytes(recv_sem, phases - 1, other_v)
    send_chips(phases - 2, lambda q: other_v.at[(slice(None), *mix_block(q))], recv_v.at[other_slots])
    recv_v[other_slots] = other_v[:, mix_rows, mix_cols]
    send_chips(0, lambda q: pack_v, bw_v.at[core, chip])
    left_mine = left_v.at[pl.ds(core * per, per)]
    send(3, left_ref, left_mine, partner)

    def into_rows(c):
        def some(q, carry):
            base = pl.multiple_of(q * 32, 32)
            both = jnp.concatenate(
                [
                    recv_v[pl.ds(c * (pairs // 2) + base + 16 * i, 16)].reshape(256, LANES)
                    for i in range(2)
                ],
                axis=1,
            )
            both = dot(swap_v[...], both).astype(BF16)
            for r in range(16):
                for i in range(2):
                    bm_v[c, pl.ds(base + 16 * i, 16), r * LANES : (r + 1) * LANES] = both[
                        16 * r : 16 * (r + 1), i * LANES : (i + 1) * LANES
                    ]
            return carry

        lax.fori_loop(0, pairs // 64, some, 0)

    def col_chunk(j):
        return pl.ds(pl.multiple_of(j * 256, 256), 256)

    arrived = recv_v.at[pl.ds(0, (chips - 1) * per)]
    loads[5].wait()
    wait_bytes(recv_sem, 1, arrived)
    into_rows(core)

    def mix_first(j, carry):
        acc_v[:, col_chunk(j)] = dot(mix_v[core], bm_v[core, :, col_chunk(j)])
        return carry

    lax.fori_loop(0, 8, mix_first, 0)
    wait_bytes(recv_sem, phases - 2, arrived)
    into_rows(1 - core)
    for i in range(2):
        rows = slice(i * (pairs // 2), (i + 1) * (pairs // 2))

        def mix_second(j, carry, rows=rows):
            ym_v[rows, col_chunk(j)] = (
                acc_v[rows, col_chunk(j)]
                + dot(mix_v[1 - core, rows, :], bm_v[1 - core, :, col_chunk(j)])
            ).astype(BF16)
            return carry

        lax.fori_loop(0, 8, mix_second, 0)

        def into_tiles(q, carry, i=i):
            base = pl.multiple_of(q * 32 + i * (pairs // 2), 32)
            both = jnp.concatenate(
                [
                    jnp.concatenate(
                        [
                            ym_v[pl.ds(base + 16 * j, 16), r * LANES : (r + 1) * LANES]
                            for r in range(16)
                        ],
                        axis=0,
                    )
                    for j in range(2)
                ],
                axis=1,
            )
            both = dot(swap_v[...], both).astype(BF16)
            for j in range(2):
                cbuf_v[pl.ds(base + 16 * j, 16)] = both[
                    :, j * LANES : (j + 1) * LANES
                ].reshape(16, 16, LANES)
            return carry

        lax.fori_loop(0, pairs // 64, into_tiles, 0)
        send_half(
            2, i, lambda q: cbuf_v.at[mix_slots(q)], comp_v.at[:, mix_rows, mix_cols]
        )
    comp_v[:, mix_rows, mix_cols] = cbuf_v[mix_slots(chip)]

    wait_bytes(recv_sem, 0, bw_v.at[0, pl.ds(0, chips - 1)])
    send(4, bw_v.at[core], bw_v.at[core], partner)
    wait_bytes(recv_sem, 4, bw_v.at[0])
    square = (256, 256)
    spread = (iota(square, 1) == spread_row(iota(square, 0))).astype(F32).astype(BF16)
    for g in range(states // 64):
        both = jnp.concatenate(
            [
                bw_v[g % 2, g // 2 * 16 : (g // 2 + 1) * 16, i].reshape(256, LANES)
                for i in range(2)
            ],
            axis=1,
        )
        both = dot(spread, both)
        for c in range(across):
            rows, cols = slice(64 * g, 64 * (g + 1)), slice(c * LANES, (c + 1) * LANES)
            mask = mask_of(
                64 * g + iota((64, 1), 0), c * LANES + iota((1, LANES), 1)
            )
            tile = both[64 * c : 64 * (c + 1)]
            u_v[rows, cols] = tile[:, :LANES].astype(BF16)
            state_v[0, c // 2, rows, c % 2 * LANES : (c % 2 + 1) * LANES] = (
                tile[:, LANES:] * mask
            ).astype(BF16)

    loads[6].wait()
    wait_bytes(recv_sem, 3, left_mine)

    def build(s, carry):
        rotated = dot(left_v[s], u_v[...]).astype(BF16)
        built_v[s] = dot(u_v[...], rotated, ((0,), (0,))).astype(BF16)
        return carry

    lax.fori_loop(0, group, build, 0)

    def apply(k, side):
        def one(s, carry):
            applied_v[s, side] = dot(built_v[s], state_v[k, side]).astype(BF16)
            return carry

        lax.fori_loop(0, group, one, 0)

    apply(0, 0)
    apply(0, 1)
    wait_bytes(recv_sem, 2, cbuf_v.at[pl.ds(0, pairs - group)])

    def term(i):
        rows = slice(i * half, (i + 1) * half)
        total = jnp.zeros((half, half), F32)
        for s in range(group):
            for side in range(2):
                total += dot(
                    applied_v[s, side, rows, :],
                    comp_v[s, :, side * half : (side + 1) * half],
                    ((1,), (1,)),
                )
        part_v[rows, :] = total.astype(BF16)

    def summed(slot):
        def some(j, carry):
            return carry + jnp.sum(rs_v[slot, pl.ds(j * 8, 8)].astype(F32), axis=0)

        return lax.fori_loop(0, chips // 8, some, jnp.zeros((ROWS, LANES), F32))

    mask = mask_of(
        lax.rem(chip, 2) * half + chip // 4 * ROWS + iota((ROWS, 1), 0),
        core * half + lax.rem(chip, 4) // 2 * LANES + iota((1, LANES), 1),
    )
    all_tiles = rs_v.at[0, pl.ds(0, chips - 1)]
    phase = 5
    pending = []
    for k in range(1, ORDER):
        slot = k - 1
        for i in range(2):
            term(i)
            send_half(
                phase, i, lambda q: part_v.at[term_block(q)], rs_v.at[slot, chip]
            )
        rs_v[slot, chip] = part_v[term_rows, term_cols]
        factor = -(step_size / k)
        wait_bytes(recv_sem, phase, all_tiles)
        new = (factor * mask * summed(slot)).astype(BF16)
        tile_v[slot] = new
        state_v[k, core, term_rows, term_cols] = new
        send_chips(
            phase + 1, lambda q: tile_v.at[slot], state_v.at[(k, core, term_rows, term_cols)]
        )
        wait_bytes(send_sem, phase, all_tiles)
        wait_bytes(recv_sem, phase + 1, all_tiles)
        send(phase + 2, state_v.at[k, core], state_v.at[k, core], partner)
        apply(k, core)
        wait_bytes(recv_sem, phase + 2, state_v.at[k, 0])
        apply(k, 1 - core)
        pending += [(phase + 1, all_tiles), (phase + 2, state_v.at[0, 0])]
        phase += 3

    slot = ORDER - 1
    gather = (iota(square, 1) == gather_row(iota(square, 0))).astype(F32).astype(BF16)
    for i in range(2):
        term(i)
        both = jnp.concatenate(
            [
                jnp.concatenate(
                    [
                        part_v[128 * y : 128 * (y + 1), c * LANES : (c + 1) * LANES]
                        for c in range(2)
                    ],
                    axis=0,
                )
                for y in (2 * i, 2 * i + 1)
            ],
            axis=1,
        )
        both = dot(gather, both).astype(BF16)
        for j in range(2):
            first = 16 * (2 * i + j)
            last_v[first : first + 16] = both[:, j * LANES : (j + 1) * LANES].reshape(
                16, 16, LANES
            )
    send_chips(phase, lambda q: last_v.at[q], rs_v.at[slot, chip])
    rs_v[slot, chip] = last_v[chip]
    own_rows = states // parts
    pick = (iota((8, states), 1) == own_rows * me + iota((8, states), 0)).astype(F32).astype(BF16)
    so_far = []
    for side in range(2):
        total = dot(pick, state_v[0, side])
        for k in range(1, ORDER):
            total += dot(pick, state_v[k, side])
        so_far.append(total)
    wait_bytes(recv_sem, phase, all_tiles)
    total = summed(slot)
    pair_v[0] = total[:8]
    pair_v[1] = total[8:]
    send(phase + 1, pair_v.at[1 - core], pair_v.at[2 + core], partner)
    pair_v[2 + core] = pair_v[core]
    wait_bytes(send_sem, phase + 1, pair_v.at[0])
    wait_bytes(recv_sem, phase + 1, pair_v.at[0])
    for side in range(2):
        from_side = pair_v[2 + side]
        for c in range(2):
            cols = slice(side * half + c * LANES, side * half + (c + 1) * LANES)
            local = slice(c * LANES, (c + 1) * LANES)
            mask = mask_of(
                own_rows * me + iota((own_rows, 1), 0),
                side * half + c * LANES + iota((1, LANES), 1),
            )
            new = -(step_size / ORDER) * mask * from_side[own_rows * c : own_rows * (c + 1)]
            out_ref[:, cols] = so_far[side][:own_rows, local] + new.astype(BF16).astype(F32)

    wait_bytes(send_sem, 0, bw_v.at[0, pl.ds(0, chips - 1)])
    for started in (1, phases - 2):
        wait_bytes(send_sem, started, arrived)
    wait_bytes(send_sem, phases - 1, other_v)
    wait_bytes(send_sem, 2, recv_v.at[pl.ds(0, pairs - group)])
    wait_bytes(send_sem, 3, left_mine)
    wait_bytes(send_sem, 4, bw_v.at[0])
    for started, ref in pending:
        wait_bytes(send_sem, started, ref)
    wait_bytes(send_sem, phase, all_tiles)


def local(site_basis, left_ops, right_ops, integrals, wavefunction, pair_order, sector_sizes):
    states = wavefunction.shape[1]
    pairs = integrals.shape[0]
    per = left_ops.shape[0]
    parts = pairs // per
    vmem = pl.BlockSpec(memory_space=pltpu.VMEM)
    anywhere = pl.BlockSpec(memory_space=pltpu.HBM)
    ops = (2 * per, states, states)
    half = states // 2
    phases = 6 + 3 * ORDER
    body = lambda *refs: kernel(*refs, states=states, pairs=pairs, parts=parts)
    return pl.pallas_call(
        body,
        out_shape=jax.ShapeDtypeStruct(wavefunction.shape, F32),
        in_specs=[anywhere] * 7,
        out_specs=vmem,
        scratch_shapes=[
            pltpu.VMEM((1, pairs), jnp.int32),
            pltpu.SMEM(sector_sizes.shape, jnp.int32),
            pltpu.VMEM(site_basis.shape, BF16),
            pltpu.VMEM(integrals.shape, BF16),
            pltpu.VMEM(wavefunction.shape, BF16),
            pltpu.VMEM(ops, BF16),
            pltpu.VMEM((2, ROWS, LANES), BF16),
            pltpu.VMEM((2, parts // 2, 2, ROWS, LANES), BF16),
            pltpu.VMEM((states, states), BF16),
            pltpu.VMEM(ops, BF16),
            pltpu.VMEM((2 * per, 2, states, half), BF16),
            pltpu.VMEM((pairs, ROWS, LANES), BF16),
            pltpu.VMEM((2, pairs // 2, ROWS * LANES), BF16),
            pltpu.VMEM((pairs, ROWS * LANES), BF16),
            pltpu.VMEM((pairs, ROWS, LANES), BF16),
            pltpu.VMEM((2 * per, half, states), BF16),
            pltpu.VMEM((2, pairs, pairs // 2), BF16),
            pltpu.VMEM((ORDER, 2, states, half), BF16),
            pltpu.VMEM((states, half), BF16),
            pltpu.VMEM((ORDER, parts // 2, ROWS, LANES), BF16),
            pltpu.VMEM((parts // 2, ROWS, LANES), BF16),
            pltpu.VMEM((ORDER, ROWS, LANES), BF16),
            pltpu.VMEM((256, 256), BF16),
            pltpu.VMEM((4, 8, LANES), F32),
            pltpu.VMEM((per, half, states), BF16),
            pltpu.VMEM((pairs, ROWS * LANES), F32),
            pltpu.SemaphoreType.DMA((7,)),
            pltpu.SemaphoreType.DMA((phases,)),
            pltpu.SemaphoreType.DMA((phases,)),
        ],
        compiler_params=pltpu.CompilerParams(
            collective_id=0, has_side_effects=True, vmem_limit_bytes=62 << 20
        ),
    )(
        pair_order.reshape(1, pairs), sector_sizes, site_basis, left_ops, right_ops,
        integrals, wavefunction,
    )


def solution(mesh):
    in_specs = (
        P(BOTH, None), P(BOTH, None, None), P(BOTH, None, None), P(), P(BOTH, None), P(), P()
    )
    return jax.shard_map(
        local, mesh=mesh, in_specs=in_specs, out_specs=P(BOTH, None), check_vma=False
    )
```

time: 142 us -> 109 us (0.77)
  Pallas kernels: 135 us -> 107 us
  local copies, waits for them, and re-layouts: 7.09 us -> 2.54 us
    pallas_call x1, Pallas kernels: 135 us -> 107 us  [local(): pl.pallas_call(body, out_shape=jax.ShapeDtypeStruct(wavefunction.shape, F...]
    unnamed x13 -> x1, local copies, waits for them, and re-layouts: 6.4 us -> 1.3 us
where the time goes in v2:
time: 109 us
  Pallas kernels  107 us (98%)
  local copies, waits for them, and re-layouts  2.54 us (2%)
    pallas_call x1, Pallas kernels, local(): pl.pallas_call(body, out_shape=jax.ShapeDtypeStruct(wavefunction.shape, F...  107 us

profile of v2, /device:TPU:1, one launch (start us, length us, event | category | flops | bytes accessed | tf_op | source)
XLA Modules:
  0.0 109.3 jit_solution(5166380529548543587)
XLA Ops:
  0.0 1.2 %reshape.3.refs_0_ = s32[1,384]{1,0:T(1,128)} reshape(s32[384]{0:T(512)} %param.12) | data formatting | bytes 3072 | tf_op jit(solution)/shard_map/reshape | solution.py:503
  1.2 106.7 %shard_map.73 = f32[4,512]{1,0:T(4,128)} custom-call(s32[1,384]{1,0:T(1,128)} %reshape.3.refs_0_, s32[8]{0:T(128)} %refs_1_.1, bf16[4,512]{1,0:T(4,128)(2,1)} %refs_2_.1, bf16[3,512,512]{2,1,0:T(8,128)(2,1)} %refs_3_.1, bf16[3,512,512]{2,1,0:T(8,128)(2,1)} %refs_4_.1, bf16[384,384]{1,0:T(8,128)(2,1)} %refs_5_.1, bf16[4,512]{1,0:T(4,128)(2,1)} %refs_6_.1), custom_call_target="tpu_custom_call" | custom-call | tf_op jit(solution)/shard_map/pallas_call | solution.py:463
  108.0 1.3 %copy.9 = f32[4,512]{1,0:T(4,128)} copy(f32[4,512]{1,0:T(4,128)} %shard_map.73) | data formatting | bytes 16384

commit v3 on v2

--- a/solution.py
+++ b/solution.py
@@ -48,12 +48,12 @@
     order_ref, sizes_ref, basis_ref, left_ref, right_ref, integrals_ref, wave_ref,
     out_ref,
     order_v, sizes_v, basis_v, integrals_v, wave_v,
-    left_v, pack_v, bw_v, u_v, built_v, applied_v, recv_v, bm_v, ym_v, cbuf_v, comp_v,
-    mix_v, state_v, part_v, rs_v, last_v, tile_v, swap_v, pair_v, other_v, acc_v, local_sem, send_sem, recv_sem,
+    left_v, pack_v, basis_all, wave_all, u_v, built_v, applied_v, recv_v, bm_v, ym_v, cbuf_v, comp_v,
+    mix_v, state_v, part_v, rs_v, last_v, tile_v, swap_v, pair_v, other_v, acc_v, meet_v, met_v, local_sem, send_sem, recv_sem,
     *, states, pairs, parts,
 ):
     per = pairs // parts
-    phases = 6 + 3 * ORDER
+    phases = 8 + 3 * ORDER
     group = 2 * per
     narrow = lax.axis_size("narrow")
     w, n = lax.axis_index("wide"), lax.axis_index("narrow")
@@ -159,7 +159,9 @@
 
     pack_v[0] = packed(basis_v)
     pack_v[1] = packed(wave_v)
-    bw_v[core, chip] = pack_v[...]
+    by_z = z * (chips // 4) + y * 4 + x
+    basis_all[core, chip] = pack_v[0]
+    wave_all[core, by_z] = pack_v[1]
     swap_v[...] = tile_swap(256)
 
     def take(ids, width):
@@ -199,6 +201,11 @@
     pl.semaphore_wait(barrier, chips)
 
     send(phases - 1, right_ref.at[:, other_half, :], other_v, partner)
+    for a in (2, 1, 3, 0):
+        for b in (2, 1, 3, 0):
+            if (a, b) != (0, 0):
+                send(0, pack_v.at[0], basis_all.at[core, chip], (w, to_x[a] + to_z[b]))
+                send(0, pack_v.at[1], wave_all.at[core, by_z], (to_w[a], to_x[b] + z))
     send_chips(
         1,
         lambda q: right_ref.at[
@@ -209,7 +216,13 @@
     wait_bytes(recv_sem, phases - 1, other_v)
     send_chips(phases - 2, lambda q: other_v.at[(slice(None), *mix_block(q))], recv_v.at[other_slots])
     recv_v[other_slots] = other_v[:, mix_rows, mix_cols]
-    send_chips(0, lambda q: pack_v, bw_v.at[core, chip])
+    plane = chips // 4
+    wait_bytes(recv_sem, 0, basis_all.at[0, pl.ds(0, 2 * plane - 2)])
+    for d in (2, 1, 3):
+        block_of_y = basis_all.at[core, pl.ds(y * plane, plane)]
+        send(4, block_of_y, block_of_y, (to_w[d], n))
+        block_of_z = wave_all.at[core, pl.ds(z * plane, plane)]
+        send(4, block_of_z, block_of_z, (w, to_x[0] + to_z[d]))
     left_mine = left_v.at[pl.ds(core * per, per)]
     send(3, left_ref, left_mine, partner)
 
@@ -231,7 +244,7 @@
                     ]
             return carry
 
-        lax.fori_loop(0, pairs // 64, some, 0)
+        lax.fori_loop(0, pairs // 64, some, 0, unroll=True)
 
     def col_chunk(j):
         return pl.ds(pl.multiple_of(j * 256, 256), 256)
@@ -245,7 +258,7 @@
         acc_v[:, col_chunk(j)] = dot(mix_v[core], bm_v[core, :, col_chunk(j)])
         return carry
 
-    lax.fori_loop(0, 8, mix_first, 0)
+    lax.fori_loop(0, 8, mix_first, 0, unroll=True)
     wait_bytes(recv_sem, phases - 2, arrived)
     into_rows(1 - core)
     for i in range(2):
@@ -258,7 +271,7 @@
             ).astype(BF16)
             return carry
 
-        lax.fori_loop(0, 8, mix_second, 0)
+        lax.fori_loop(0, 8, mix_second, 0, unroll=True)
 
         def into_tiles(q, carry, i=i):
             base = pl.multiple_of(q * 32 + i * (pairs // 2), 32)
@@ -282,22 +295,27 @@
                 ].reshape(16, 16, LANES)
             return carry
 
-        lax.fori_loop(0, pairs // 64, into_tiles, 0)
+        lax.fori_loop(0, pairs // 64, into_tiles, 0, unroll=True)
         send_half(
             2, i, lambda q: cbuf_v.at[mix_slots(q)], comp_v.at[:, mix_rows, mix_cols]
         )
     comp_v[:, mix_rows, mix_cols] = cbuf_v[mix_slots(chip)]
 
-    wait_bytes(recv_sem, 0, bw_v.at[0, pl.ds(0, chips - 1)])
-    send(4, bw_v.at[core], bw_v.at[core], partner)
-    wait_bytes(recv_sem, 4, bw_v.at[0])
+    wait_bytes(recv_sem, 4, recv_v.at[pl.ds(0, 6 * plane)])
+    send(phases - 3, basis_all.at[core], basis_all.at[core], partner)
+    send(phases - 4, wave_all.at[core], wave_all.at[core], partner)
+    wait_bytes(recv_sem, phases - 3, basis_all.at[0])
+    wait_bytes(recv_sem, phases - 4, wave_all.at[0])
     square = (256, 256)
     spread = (iota(square, 1) == spread_row(iota(square, 0))).astype(F32).astype(BF16)
     for g in range(states // 64):
+        waves = [
+            wave_all[g % 2, (i % 4) * plane + g // 2 * 4 + i // 4] for i in range(plane)
+        ]
         both = jnp.concatenate(
             [
-                bw_v[g % 2, g // 2 * 16 : (g // 2 + 1) * 16, i].reshape(256, LANES)
-                for i in range(2)
+                basis_all[g % 2, g // 2 * plane : (g // 2 + 1) * plane].reshape(256, LANES),
+                jnp.concatenate(waves, axis=0),
             ],
             axis=1,
         )
@@ -323,18 +341,42 @@
 
     lax.fori_loop(0, group, build, 0)
 
-    def apply(k, side):
+    def apply(s, carry):
+        for side in range(2):
+            applied_v[s, side] = dot(built_v[s], state_v[0, side]).astype(BF16)
+        return carry
+
+    lax.fori_loop(0, group, apply, 0)
+    wait_bytes(recv_sem, 2, cbuf_v.at[pl.ds(0, pairs - group)])
+
+    def mine_of(side):
+        return pl.ds(pl.multiple_of(side * half, half), half)
+
+    def meet_own(k):
         def one(s, carry):
-            applied_v[s, side] = dot(built_v[s], state_v[k, side]).astype(BF16)
+            meet_v[s] = dot(state_v[k, core], comp_v[s, :, mine_of(core)], ((1,), (1,)))
             return carry
 
-        lax.fori_loop(0, group, one, 0)
-
-    apply(0, 0)
-    apply(0, 1)
-    wait_bytes(recv_sem, 2, cbuf_v.at[pl.ds(0, pairs - group)])
-
-    def term(i):
+        lax.fori_loop(0, group, one, 0, unroll=True)
+
+    def meet_other(k):
+        def one(s, carry):
+            met_v[s] = (
+                meet_v[s]
+                + dot(state_v[k, 1 - core], comp_v[s, :, mine_of(1 - core)], ((1,), (1,)))
+            ).astype(BF16)
+            return carry
+
+        lax.fori_loop(0, group, one, 0, unroll=True)
+
+    def later_term(i):
+        rows = slice(i * half, (i + 1) * half)
+        total = dot(built_v[0, rows, :], met_v[0])
+        for s in range(1, group):
+            total += dot(built_v[s, rows, :], met_v[s])
+        part_v[rows, :] = total.astype(BF16)
+
+    def first_term(i):
         rows = slice(i * half, (i + 1) * half)
         total = jnp.zeros((half, half), F32)
         for s in range(group):
@@ -350,7 +392,7 @@
         def some(j, carry):
             return carry + jnp.sum(rs_v[slot, pl.ds(j * 8, 8)].astype(F32), axis=0)
 
-        return lax.fori_loop(0, chips // 8, some, jnp.zeros((ROWS, LANES), F32))
+        return lax.fori_loop(0, chips // 8, some, jnp.zeros((ROWS, LANES), F32), unroll=True)
 
     mask = mask_of(
         lax.rem(chip, 2) * half + chip // 4 * ROWS + iota((ROWS, 1), 0),
@@ -362,7 +404,7 @@
     for k in range(1, ORDER):
         slot = k - 1
         for i in range(2):
-            term(i)
+            first_term(i) if k == 1 else later_term(i)
             send_half(
                 phase, i, lambda q: part_v.at[term_block(q)], rs_v.at[slot, chip]
             )
@@ -378,16 +420,16 @@
         wait_bytes(send_sem, phase, all_tiles)
         wait_bytes(recv_sem, phase + 1, all_tiles)
         send(phase + 2, state_v.at[k, core], state_v.at[k, core], partner)
-        apply(k, core)
+        meet_own(k)
         wait_bytes(recv_sem, phase + 2, state_v.at[k, 0])
-        apply(k, 1 - core)
+        meet_other(k)
         pending += [(phase + 1, all_tiles), (phase + 2, state_v.at[0, 0])]
         phase += 3
 
     slot = ORDER - 1
     gather = (iota(square, 1) == gather_row(iota(square, 0))).astype(F32).astype(BF16)
     for i in range(2):
-        term(i)
+        later_term(i)
         both = jnp.concatenate(
             [
                 jnp.concatenate(
@@ -407,7 +449,20 @@
             last_v[first : first + 16] = both[:, j * LANES : (j + 1) * LANES].reshape(
                 16, 16, LANES
             )
-    send_chips(phase, lambda q: last_v.at[q], rs_v.at[slot, chip])
+        for j in (2 * i, 2 * i + 1):
+            for a in (2, 1, 3, 0):
+                for b in (2, 1, 3, 0):
+                    to_n = to_x[a] + to_z[b]
+                    device = (2 * j + core, to_n)
+                    from_tile = last_v.at[j * narrow + to_n]
+                    if (a, b) == (0, 0):
+
+                        @pl.when(y != j)
+                        def _():
+                            send(phase, from_tile, rs_v.at[slot, chip], device)
+
+                    else:
+                        send(phase, from_tile, rs_v.at[slot, chip], device)
     rs_v[slot, chip] = last_v[chip]
     own_rows = states // parts
     pick = (iota((8, states), 1) == own_rows * me + iota((8, states), 0)).astype(F32).astype(BF16)
@@ -437,13 +492,15 @@
             new = -(step_size / ORDER) * mask * from_side[own_rows * c : own_rows * (c + 1)]
             out_ref[:, cols] = so_far[side][:own_rows, local] + new.astype(BF16).astype(F32)
 
-    wait_bytes(send_sem, 0, bw_v.at[0, pl.ds(0, chips - 1)])
+    wait_bytes(send_sem, 0, basis_all.at[0, pl.ds(0, 2 * plane - 2)])
     for started in (1, phases - 2):
         wait_bytes(send_sem, started, arrived)
     wait_bytes(send_sem, phases - 1, other_v)
     wait_bytes(send_sem, 2, recv_v.at[pl.ds(0, pairs - group)])
     wait_bytes(send_sem, 3, left_mine)
-    wait_bytes(send_sem, 4, bw_v.at[0])
+    wait_bytes(send_sem, 4, recv_v.at[pl.ds(0, 6 * plane)])
+    wait_bytes(send_sem, phases - 3, basis_all.at[0])
+    wait_bytes(send_sem, phases - 4, wave_all.at[0])
     for started, ref in pending:
         wait_bytes(send_sem, started, ref)
     wait_bytes(send_sem, phase, all_tiles)
@@ -458,7 +515,7 @@
     anywhere = pl.BlockSpec(memory_space=pltpu.HBM)
     ops = (2 * per, states, states)
     half = states // 2
-    phases = 6 + 3 * ORDER
+    phases = 8 + 3 * ORDER
     body = lambda *refs: kernel(*refs, states=states, pairs=pairs, parts=parts)
     return pl.pallas_call(
         body,
@@ -473,7 +530,8 @@
             pltpu.VMEM(wavefunction.shape, BF16),
             pltpu.VMEM(ops, BF16),
             pltpu.VMEM((2, ROWS, LANES), BF16),
-            pltpu.VMEM((2, parts // 2, 2, ROWS, LANES), BF16),
+            pltpu.VMEM((2, parts // 2, ROWS, LANES), BF16),
+            pltpu.VMEM((2, parts // 2, ROWS, LANES), BF16),
             pltpu.VMEM((states, states), BF16),
             pltpu.VMEM(ops, BF16),
             pltpu.VMEM((2 * per, 2, states, half), BF16),
@@ -492,6 +550,8 @@
             pltpu.VMEM((4, 8, LANES), F32),
             pltpu.VMEM((per, half, states), BF16),
             pltpu.VMEM((pairs, ROWS * LANES), F32),
+            pltpu.VMEM((2 * per, states, half), F32),
+            pltpu.VMEM((2 * per, states, half), BF16),
             pltpu.SemaphoreType.DMA((7,)),
             pltpu.SemaphoreType.DMA((phases,)),
             pltpu.SemaphoreType.DMA((phases,)),

time: 109 us -> 102 us (0.936)
  Pallas kernels: 107 us -> 99.2 us
    pallas_call x1, Pallas kernels: 107 us -> 99.2 us  [local(): pl.pallas_call(body, out_shape=jax.ShapeDtypeStruct(wavefunction.shape, F...]
where the time goes in v3:
time: 102 us
  Pallas kernels  99.2 us (97%)
  local copies, waits for them, and re-layouts  2.54 us (2%)
    pallas_call x1, Pallas kernels, local(): pl.pallas_call(body, out_shape=jax.ShapeDtypeStruct(wavefunction.shape, F...  99.2 us

profile of v3, /device:TPU:1, one launch (start us, length us, event | category | flops | bytes accessed | tf_op | source)
XLA Modules:
  0.0 101.7 jit_solution(9571815223040242101)
XLA Ops:
  0.0 1.2 %reshape.3.refs_0_ = s32[1,384]{1,0:T(1,128)} reshape(s32[384]{0:T(512)} %param.12) | data formatting | bytes 3072 | tf_op jit(solution)/shard_map/reshape | solution.py:563
  1.2 99.2 %shard_map.73 = f32[4,512]{1,0:T(4,128)} custom-call(s32[1,384]{1,0:T(1,128)} %reshape.3.refs_0_, s32[8]{0:T(128)} %refs_1_.1, bf16[4,512]{1,0:T(4,128)(2,1)} %refs_2_.1, bf16[3,512,512]{2,1,0:T(8,128)(2,1)} %refs_3_.1, bf16[3,512,512]{2,1,0:T(8,128)(2,1)} %refs_4_.1, bf16[384,384]{1,0:T(8,128)(2,1)} %refs_5_.1, bf16[4,512]{1,0:T(4,128)(2,1)} %refs_6_.1), custom_call_target="tpu_custom_call" | custom-call | tf_op jit(solution)/shard_map/pallas_call | solution.py:520
  100.4 1.3 %copy.9 = f32[4,512]{1,0:T(4,128)} copy(f32[4,512]{1,0:T(4,128)} %shard_map.73) | data formatting | bytes 16384

commit v4 on v3

--- a/solution.py
+++ b/solution.py
@@ -85,37 +85,42 @@
     def term_block(q):
         return block(lax.rem(q, 2) * (chips // 4) + lax.div(q, 4), lax.div(lax.rem(q, 4), 2))
 
-    def mix_slots(q):
-        return pl.ds((lax.rem(q, 2) * (chips // 2) + lax.div(q, 2)) * group, group)
-
     def send(phase, src, dst, device):
         pltpu.make_async_remote_copy(
             src_ref=src, dst_ref=dst, send_sem=send_sem.at[phase],
             recv_sem=recv_sem.at[phase], device_id=device, device_id_type=MESH,
         ).start()
 
+    to_n = [[i + j for j in to_z] for i in to_x]
+    reached = [
+        (to_y[dy] + to_n[dx][dz], (to_w[dy], to_n[dx][dz])) for dy, dx, dz in far_first(4)
+    ]
+
     def each_chip(visit):
-        to_n = [[i + j for j in to_z] for i in to_x]
-        for dy, dx, dz in far_first(4):
-            if (dy, dx, dz) != (0, 0, 0):
-                visit(to_y[dy] + to_n[dx][dz], (to_w[dy], to_n[dx][dz]))
+        for q, device in reached[:-1]:
+            visit(q, device)
 
     def send_chips(phase, src, dst):
         each_chip(lambda q, device: send(phase, src(q), dst, device))
 
-    def send_half(phase, parity, src, dst):
+    turn = lax.rem(x + y + z, 2)
+
+    def send_half(phase, parity, dst):
         first = lax.rem(parity + z, 2)
-        to_n = [[i + lax.rem(z + first + 2 * j, 4) for j in range(2)] for i in to_x]
+        at_z = [lax.rem(z + first + 2 * j, 4) for j in range(2)]
+        half_z = [lax.div(j, 2) for j in at_z]
+        at_yx = [[lax.div(i + j, 4) for j in to_x] for i in to_y]
         for dy, dx, dz in far_first(2):
-            q, device = to_y[dy] + to_n[dx][dz], (to_w[dy], to_n[dx][dz])
+            src = part_v.at[parity, half_z[dz], at_yx[dy][dx]]
+            device = (to_w[dy], to_x[dx] + at_z[dz])
             if (dy, dx, dz) == (0, 0, 0):
 
                 @pl.when(first == 1)
                 def _():
-                    send(phase, src(q), dst, device)
+                    send(phase, src, dst, device)
 
             else:
-                send(phase, src(q), dst, device)
+                send(phase, src, dst, device)
 
     def wait_bytes(sem, phase, ref):
         pltpu.make_async_copy(ref, ref, sem.at[phase]).wait()
@@ -175,7 +180,9 @@
     owner = (place * (65536 // group + 1)) >> 16
     rest = place - owner * group
     of_core = (rest >= per).astype(jnp.int32)
-    owner = (owner & (chips // 2 - 1)) * 2 + owner // (chips // 2)
+    order_of_owners = owner
+    for i, (q, _) in enumerate(reached):
+        owner = jnp.where(order_of_owners == i, q, owner)
     by_row = dot(chosen, take(slot(owner, of_core, rest - of_core * per), pairs)).astype(BF16)
     place = iota((1, pairs // 2), 1)
     sender = (place * (65536 // per + 1)) >> 16
@@ -296,10 +303,14 @@
             return carry
 
         lax.fori_loop(0, pairs // 64, into_tiles, 0, unroll=True)
-        send_half(
-            2, i, lambda q: cbuf_v.at[mix_slots(q)], comp_v.at[:, mix_rows, mix_cols]
-        )
-    comp_v[:, mix_rows, mix_cols] = cbuf_v[mix_slots(chip)]
+        for j in range(i * (chips // 2), min((i + 1) * (chips // 2), chips - 1)):
+            send(
+                2,
+                cbuf_v.at[pl.ds(j * group, group)],
+                comp_v.at[:, mix_rows, mix_cols],
+                reached[j][1],
+            )
+    comp_v[:, mix_rows, mix_cols] = cbuf_v[pairs - group :]
 
     wait_bytes(recv_sem, 4, recv_v.at[pl.ds(0, 6 * plane)])
     send(phases - 3, basis_all.at[core], basis_all.at[core], partner)
@@ -369,24 +380,25 @@
 
         lax.fori_loop(0, group, one, 0, unroll=True)
 
+    def rows_of(i):
+        return pl.ds(pl.multiple_of(i * half, half), half)
+
     def later_term(i):
-        rows = slice(i * half, (i + 1) * half)
-        total = dot(built_v[0, rows, :], met_v[0])
+        total = dot(built_v[0, rows_of(i), :], met_v[0])
         for s in range(1, group):
-            total += dot(built_v[s, rows, :], met_v[s])
-        part_v[rows, :] = total.astype(BF16)
+            total += dot(built_v[s, rows_of(i), :], met_v[s])
+        return total.astype(BF16)
 
     def first_term(i):
-        rows = slice(i * half, (i + 1) * half)
         total = jnp.zeros((half, half), F32)
         for s in range(group):
             for side in range(2):
                 total += dot(
-                    applied_v[s, side, rows, :],
+                    applied_v[s, side, rows_of(i), :],
                     comp_v[s, :, side * half : (side + 1) * half],
                     ((1,), (1,)),
                 )
-        part_v[rows, :] = total.astype(BF16)
+        return total.astype(BF16)
 
     def summed(slot):
         def some(j, carry):
@@ -403,12 +415,15 @@
     pending = []
     for k in range(1, ORDER):
         slot = k - 1
-        for i in range(2):
-            first_term(i) if k == 1 else later_term(i)
-            send_half(
-                phase, i, lambda q: part_v.at[term_block(q)], rs_v.at[slot, chip]
-            )
-        rs_v[slot, chip] = part_v[term_rows, term_cols]
+        for j in range(2):
+            parity = lax.rem(turn + j, 2)
+            partial = first_term(parity) if k == 1 else later_term(parity)
+            for c in range(2):
+                part_v[parity, c] = partial[:, c * LANES : (c + 1) * LANES].reshape(
+                    chips // 4, ROWS, LANES
+                )
+            send_half(phase, parity, rs_v.at[slot, chip])
+        rs_v[slot, chip] = part_v[lax.rem(z, 2), lax.div(z, 2), lax.div(chip, 4)]
         factor = -(step_size / k)
         wait_bytes(recv_sem, phase, all_tiles)
         new = (factor * mask * summed(slot)).astype(BF16)
@@ -429,41 +444,40 @@
     slot = ORDER - 1
     gather = (iota(square, 1) == gather_row(iota(square, 0))).astype(F32).astype(BF16)
     for i in range(2):
-        later_term(i)
+        upper = lax.rem(turn + i, 2)
+        partial = later_term(upper)
         both = jnp.concatenate(
             [
                 jnp.concatenate(
                     [
-                        part_v[128 * y : 128 * (y + 1), c * LANES : (c + 1) * LANES]
+                        partial[128 * j : 128 * (j + 1), c * LANES : (c + 1) * LANES]
                         for c in range(2)
                     ],
                     axis=0,
                 )
-                for y in (2 * i, 2 * i + 1)
+                for j in range(2)
             ],
             axis=1,
         )
         both = dot(gather, both).astype(BF16)
         for j in range(2):
-            first = 16 * (2 * i + j)
-            last_v[first : first + 16] = both[:, j * LANES : (j + 1) * LANES].reshape(
-                16, 16, LANES
-            )
-        for j in (2 * i, 2 * i + 1):
+            at_y = 2 * upper + j
+            last_v[at_y] = both[:, j * LANES : (j + 1) * LANES].reshape(16, 16, LANES)
+        for j in range(2):
+            at_y = 2 * upper + j
             for a in (2, 1, 3, 0):
                 for b in (2, 1, 3, 0):
-                    to_n = to_x[a] + to_z[b]
-                    device = (2 * j + core, to_n)
-                    from_tile = last_v.at[j * narrow + to_n]
+                    device = (2 * at_y + core, to_n[a][b])
+                    from_tile = last_v.at[at_y, to_n[a][b]]
                     if (a, b) == (0, 0):
 
-                        @pl.when(y != j)
+                        @pl.when(y != at_y)
                         def _():
                             send(phase, from_tile, rs_v.at[slot, chip], device)
 
                     else:
                         send(phase, from_tile, rs_v.at[slot, chip], device)
-    rs_v[slot, chip] = last_v[chip]
+    rs_v[slot, chip] = last_v[y, n]
     own_rows = states // parts
     pick = (iota((8, states), 1) == own_rows * me + iota((8, states), 0)).astype(F32).astype(BF16)
     so_far = []
@@ -542,9 +556,9 @@
             pltpu.VMEM((2 * per, half, states), BF16),
             pltpu.VMEM((2, pairs, pairs // 2), BF16),
             pltpu.VMEM((ORDER, 2, states, half), BF16),
-            pltpu.VMEM((states, half), BF16),
+            pltpu.VMEM((2, 2, parts // 8, ROWS, LANES), BF16),
             pltpu.VMEM((ORDER, parts // 2, ROWS, LANES), BF16),
-            pltpu.VMEM((parts // 2, ROWS, LANES), BF16),
+            pltpu.VMEM((4, parts // 8, ROWS, LANES), BF16),
             pltpu.VMEM((ORDER, ROWS, LANES), BF16),
             pltpu.VMEM((256, 256), BF16),
             pltpu.VMEM((4, 8, LANES), F32),

time: 102 us -> 98.3 us (0.964)
  Pallas kernels: 99.2 us -> 95.6 us
    pallas_call x1, Pallas kernels: 99.2 us -> 95.6 us  [local(): pl.pallas_call(body, out_shape=jax.ShapeDtypeStruct(wavefunction.shape, F...]
where the time goes in v4:
time: 98.3 us; the launch traced here: 98.1 us
  Pallas kernels  95.6 us (97%)
  local copies, waits for them, and re-layouts  2.54 us (3%)
    pallas_call x1, Pallas kernels, local(): pl.pallas_call(body, out_shape=jax.ShapeDtypeStruct(wavefunction.shape, F...  95.6 us

profile of v4, /device:TPU:1, one launch (start us, length us, event | category | flops | bytes accessed | tf_op | source)
XLA Modules:
  0.0 98.1 jit_solution(13996248280503814433)
XLA Ops:
  0.0 1.2 %reshape.3.refs_0_ = s32[1,384]{1,0:T(1,128)} reshape(s32[384]{0:T(512)} %param.12) | data formatting | bytes 3072 | tf_op jit(solution)/shard_map/reshape | solution.py:577
  1.2 95.6 %shard_map.73 = f32[4,512]{1,0:T(4,128)} custom-call(s32[1,384]{1,0:T(1,128)} %reshape.3.refs_0_, s32[8]{0:T(128)} %refs_1_.1, bf16[4,512]{1,0:T(4,128)(2,1)} %refs_2_.1, bf16[3,512,512]{2,1,0:T(8,128)(2,1)} %refs_3_.1, bf16[3,512,512]{2,1,0:T(8,128)(2,1)} %refs_4_.1, bf16[384,384]{1,0:T(8,128)(2,1)} %refs_5_.1, bf16[4,512]{1,0:T(4,128)(2,1)} %refs_6_.1), custom_call_target="tpu_custom_call" | custom-call | tf_op jit(solution)/shard_map/pallas_call | solution.py:534
  96.8 1.3 %copy.9 = f32[4,512]{1,0:T(4,128)} copy(f32[4,512]{1,0:T(4,128)} %shard_map.73) | data formatting | bytes 16384
